TPU v7x, 256 devices: a whole 4x4x8 slice. The times are simulated.
256 devices in a mesh: segment: 2 (over core), et: 128 (over x, y, z).
Axes of the slice: x: 4, y: 4, z: 8, core: 2. Of those that a mesh axis runs over, the one named last changes fastest.
Arguments:
- inputs: bfloat16 [1, 128, 6144], P(None, 'et'), may hold values from -6 to 6
- cotangent: bfloat16 [1, 128, 6144], P(None, 'et'), may hold values from -6 to 6
- gate_weight: bfloat16 [2, 6144, 16384], P('segment', None, 'et'), may hold values from -0.078125 to 0.078125
- up_weight: bfloat16 [2, 6144, 16384], P('segment', None, 'et'), may hold values from -0.078125 to 0.078125
- down_weight: bfloat16 [2, 16384, 6144], P('segment', 'et'), may hold values from -0.0625 to 0.0625
- route_rows: int32 [2, 1, 128], P('segment'), may hold values from 0 to 127, as said below
- route_count: int32 [2, 1], P('segment'), may hold values from 32 to 128, as said below
- route_weight: float32 [2, 1, 128], P('segment'), may hold values from 0.05 to 1
- width_mask: int32 [2, 128], P('segment', 'et'), may hold values from 0 to 1, as said below
Outputs:
- section_output: bfloat16 [2, 1, 128, 6144], P('segment', None, 'et')
- grad_input: bfloat16 [2, 1, 128, 6144], P('segment', None, 'et')
- grad_gate: bfloat16 [2, 6144, 16384], P('segment', None, 'et')
- grad_up: bfloat16 [2, 6144, 16384], P('segment', None, 'et')
- grad_down: bfloat16 [2, 16384, 6144], P('segment', 'et')
Inputs may be any that keep to these rules, and one draw needn't show every extreme that they name: `route_rows`: each list names every one of the 128 tokens once; its first route_count entries are the slots routed to the expert. `route_count`: 128 in at least one entry. `width_mask`: the kept tiles of each section are its first ones, at least 32 of them and never all.
All inputs are finite; a program needn't handle non-finite values.
Results may differ from a plain program's by a relative error of at most 0.015.
Values may be sent and summed in bfloat16 or wider, within the bound.
No kernel may reach another device: no remote copies, remote signals or barrier semaphores. Data moves between devices by JAX's collectives and lax.ppermute only.
A program may use at most 128 MiB of HBM per device.

v0:
```python
import jax
import jax.numpy as jnp
from jax import lax
from jax.sharding import PartitionSpec as P


def shifted(value, axis, by):
    size = lax.axis_size(axis)
    pairs = [(i, i + by) for i in range(size) if 0 <= i + by < size]
    return lax.ppermute(value, axis, pairs)


def expert_hidden(picked, gate_w, up_w, keep):
    gate_value = jnp.dot(picked, gate_w, preferred_element_type=jnp.float32)
    up_value = jnp.dot(picked, up_w, preferred_element_type=jnp.float32)
    hidden = (gate_value * jax.nn.sigmoid(gate_value) * up_value * keep).astype(jnp.bfloat16)
    return (gate_value, up_value, hidden)


def expert_deltas(picked, slot_grad_in, gate_value, up_value, hidden, down_w, keep):
    contract_last = (((1,), (1,)), ((), ()))
    contract_first = (((0,), (0,)), ((), ()))
    hidden_delta = lax.dot_general(
        slot_grad_in, down_w, contract_last, preferred_element_type=jnp.float32
    )
    sig_gate = jax.nn.sigmoid(gate_value)
    gate_delta = (
        hidden_delta * keep * up_value * sig_gate * (1.0 + gate_value * (1.0 - sig_gate))
    ).astype(jnp.bfloat16)
    up_delta = (hidden_delta * keep * gate_value * sig_gate).astype(jnp.bfloat16)
    grad_gate = lax.dot_general(
        picked, gate_delta, contract_first, preferred_element_type=jnp.float32
    )
    grad_up = lax.dot_general(picked, up_delta, contract_first, preferred_element_type=jnp.float32)
    grad_down = lax.dot_general(
        hidden, slot_grad_in, contract_first, preferred_element_type=jnp.float32
    )
    return (gate_delta, up_delta, grad_gate, grad_up, grad_down)


def slot_gradient(gate_delta, up_delta, gate_w, up_w):
    contract_last = (((1,), (1,)), ((), ()))
    slot_grad = lax.dot_general(
        gate_delta, gate_w, contract_last, preferred_element_type=jnp.float32
    )
    return slot_grad + lax.dot_general(
        up_delta, up_w, contract_last, preferred_element_type=jnp.float32
    )


def take_micro(buffer, micro_index):
    return lax.dynamic_index_in_dim(buffer, micro_index, 0, keepdims=False)


def store_micro(buffer, micro_index, value):
    return lax.dynamic_update_index_in_dim(buffer, value, micro_index, 0)


def pick_route(route_rows, route_count, route_weight, micro_index):
    slot_rows = take_micro(route_rows[0], micro_index)
    live_count = take_micro(route_count[0], micro_index)
    slot_weight = take_micro(route_weight[0], micro_index)
    slot_total = slot_rows.shape[0]
    positions = jnp.arange(slot_total, dtype=jnp.int32)
    live = positions < live_count
    inverse = jnp.zeros((slot_total,), jnp.int32).at[slot_rows].set(positions)
    return (slot_rows, jnp.where(live, slot_weight, 0.0), inverse)


def per_device(
    inputs,
    cotangent,
    gate_weight,
    up_weight,
    down_weight,
    route_rows,
    route_count,
    route_weight,
    width_mask,
):
    micro_count = inputs.shape[0]
    token_rows = inputs.shape[1]
    width = inputs.shape[2]
    segment_count = lax.axis_size("segment")
    segment_index = lax.axis_index("segment")
    total_rows = token_rows * lax.axis_size("et")
    slot_count = route_rows.shape[2]
    gate_w = gate_weight[0]
    up_w = up_weight[0]
    down_w = down_weight[0]
    hidden_cols = gate_w.shape[1]
    keep = jnp.repeat(width_mask[0].astype(jnp.float32), hidden_cols // width_mask.shape[1])
    phases = micro_count + segment_count - 1
    saved_input = jnp.zeros((micro_count, token_rows, width), jnp.bfloat16)
    saved_whole = jnp.zeros((micro_count, total_rows, width), jnp.bfloat16)
    saved_gate = jnp.zeros((micro_count, slot_count, hidden_cols), jnp.float32)
    saved_up = jnp.zeros((micro_count, slot_count, hidden_cols), jnp.float32)
    saved_hidden = jnp.zeros((micro_count, slot_count, hidden_cols), jnp.bfloat16)
    outputs = jnp.zeros((micro_count, token_rows, width), jnp.bfloat16)
    incoming = jnp.zeros((token_rows, width), jnp.bfloat16)
    for phase in range(phases):
        micro_raw = phase - segment_index
        valid = (micro_raw >= 0) & (micro_raw < micro_count)
        micro_index = jnp.clip(micro_raw, 0, micro_count - 1)
        current = jnp.where(segment_index == 0, take_micro(inputs, micro_index), incoming)
        gathered = lax.all_gather(current, "et", axis=0, tiled=True)
        slot_rows, slot_scale, inverse = pick_route(
            route_rows, route_count, route_weight, micro_index
        )
        picked = jnp.take(gathered, slot_rows, axis=0)
        gate_value, up_value, hidden = expert_hidden(picked, gate_w, up_w, keep)
        outcome = jnp.dot(hidden, down_w, preferred_element_type=jnp.float32)
        added = jnp.take(slot_scale[:, None] * outcome, inverse, axis=0)
        mine = lax.psum_scatter(added, "et", scatter_dimension=0, tiled=True)
        result = (current.astype(jnp.float32) + mine).astype(jnp.bfloat16)
        late = micro_raw >= 0
        stored = jnp.where(late, micro_index, micro_count - 1)
        saved_input = store_micro(saved_input, stored, current)
        saved_whole = store_micro(saved_whole, stored, gathered)
        saved_gate = store_micro(saved_gate, stored, gate_value)
        saved_up = store_micro(saved_up, stored, up_value)
        saved_hidden = store_micro(saved_hidden, stored, hidden)
        outputs = jnp.where(valid, store_micro(outputs, micro_index, result), outputs)
        if phase + 1 < phases:
            incoming = shifted(result, "segment", 1)
    acc_gate = jnp.zeros((width, hidden_cols), jnp.float32)
    acc_up = jnp.zeros((width, hidden_cols), jnp.float32)
    acc_down = jnp.zeros((hidden_cols, width), jnp.float32)
    grad_inputs = jnp.zeros((micro_count, token_rows, width), jnp.bfloat16)
    incoming = jnp.zeros((token_rows, width), jnp.bfloat16)
    for phase in range(phases):
        micro_raw = phase - (segment_count - 1 - segment_index)
        valid = (micro_raw >= 0) & (micro_raw < micro_count)
        micro_index = jnp.clip(micro_raw, 0, micro_count - 1)
        upstream = jnp.where(
            segment_index == segment_count - 1, take_micro(cotangent, micro_index), incoming
        )
        grad_gathered = lax.all_gather(upstream, "et", axis=0, tiled=True)
        gathered = take_micro(saved_whole, micro_index)
        slot_rows, slot_scale, inverse = pick_route(
            route_rows, route_count, route_weight, micro_index
        )
        slot_scale = jnp.where(valid, slot_scale, 0.0)
        picked = jnp.take(gathered, slot_rows, axis=0)
        grad_picked = jnp.take(grad_gathered, slot_rows, axis=0)
        slot_grad_in = (slot_scale[:, None] * grad_picked.astype(jnp.float32)).astype(jnp.bfloat16)
        gate_delta, up_delta, part_gate, part_up, part_down = expert_deltas(
            picked,
            slot_grad_in,
            take_micro(saved_gate, micro_index),
            take_micro(saved_up, micro_index),
            take_micro(saved_hidden, micro_index),
            down_w,
            keep,
        )
        acc_gate = acc_gate + part_gate
        acc_up = acc_up + part_up
        acc_down = acc_down + part_down
        slot_grad = slot_gradient(gate_delta, up_delta, gate_w, up_w)
        added = jnp.take(slot_grad, inverse, axis=0)
        mine = lax.psum_scatter(added, "et", scatter_dimension=0, tiled=True)
        result = (upstream.astype(jnp.float32) + mine).astype(jnp.bfloat16)
        grad_inputs = jnp.where(valid, store_micro(grad_inputs, micro_index, result), grad_inputs)
        if phase + 1 < phases:
            incoming = shifted(result, "segment", -1)
    return (
        outputs[None],
        grad_inputs[None],
        acc_gate.astype(jnp.bfloat16)[None],
        acc_up.astype(jnp.bfloat16)[None],
        acc_down.astype(jnp.bfloat16)[None],
    )


def solution(mesh):
    return jax.shard_map(
        per_device,
        mesh=mesh,
        in_specs=(
            P(None, "et", None),
            P(None, "et", None),
            P("segment", None, "et"),
            P("segment", None, "et"),
            P("segment", "et", None),
            P("segment", None, None),
            P("segment", None),
            P("segment", None, None),
            P("segment", "et"),
        ),
        out_specs=(
            P("segment", None, "et", None),
            P("segment", None, "et", None),
            P("segment", None, "et"),
            P("segment", None, "et"),
            P("segment", "et", None),
        ),
        check_vma=False,
    )
```

profile of v0, /device:TPU:1, one launch (start us, length us, event | category | flops | bytes accessed | tf_op | source)
XLA Modules:
  0.0 1269.3 jit_solution(9324662932709823214)
XLA Ops:
  13.8 113.3 %all-gather.9.cloned.1.call-done = bf16[128,1,6144]{2,1,0:T(2,128)(2,1)} async-done(((bf16[1,1,6144]{2,1,0:T(2,128)(2,1)}), bf16[128,1,6144]{2,1,0:T(2,128)(2,1)}) %all-gather.9.cloned.1.call-update) | async-done | bytes 1572880 | tf_op jit(solution)/shard_map/all_gather | solution.py:106
  127.1 2.8 copy.25
  129.9 2.6 gather_fusion
  132.5 2.6 fusion.24
  135.1 4.2 convolution_multiply_fusion.1
  139.3 6.5 gather_fusion.1
  145.8 4.0 broadcast_select_fusion.3
  151.8 226.8 %all-reduce.9.cloned.1.call-done = f32[128,6144]{1,0:T(8,128)} async-done(((f32[128,6144]{1,0:T(8,128)}), f32[128,6144]{1,0:T(8,128)}) %all-reduce.9.cloned.1.call-update) | async-done | bytes 3145744
  381.4 4.8 collective-permute-done
  387.1 108.1 %all-gather.13.cloned.1.call-done = bf16[128,1,6144]{2,1,0:T(2,128)(2,1)} async-done(((bf16[1,1,6144]{2,1,0:T(2,128)(2,1)}), bf16[128,1,6144]{2,1,0:T(2,128)(2,1)}) %all-gather.13.cloned.1.call-update) | async-done | bytes 1572880 | tf_op jit(solution)/shard_map/all_gather | solution.py:138
  495.3 2.8 copy.23
  498.1 2.6 gather_fusion.4
  500.7 111.6 %all-gather.11.cloned.1.call-done = bf16[128,1,6144]{2,1,0:T(2,128)(2,1)} async-done(((bf16[1,1,6144]{2,1,0:T(2,128)(2,1)}), bf16[128,1,6144]{2,1,0:T(2,128)(2,1)}) %all-gather.11.cloned.1.call-update) | async-done | bytes 1572880 | tf_op jit(solution)/shard_map/all_gather | solution.py:106
  612.3 2.8 copy.24
  615.1 2.6 gather_fusion.2
  617.7 2.2 fusion.14
  623.2 2.3 convolution_add_fusion.4
  625.5 6.5 gather_fusion.5
  632.0 4.0 broadcast_select_fusion.1
  636.0 228.9 %all-reduce.11.cloned.1.call-done = f32[128,6144]{1,0:T(8,128)} async-done(((f32[128,6144]{1,0:T(8,128)}), f32[128,6144]{1,0:T(8,128)}) %all-reduce.11.cloned.1.call-update) | async-done | bytes 3145744
  866.5 6.0 collective-permute-start.1
  874.3 107.9 %all-gather.15.cloned.1.call-done = bf16[128,1,6144]{2,1,0:T(2,128)(2,1)} async-done(((bf16[1,1,6144]{2,1,0:T(2,128)(2,1)}), bf16[128,1,6144]{2,1,0:T(2,128)(2,1)}) %all-gather.15.cloned.1.call-update) | async-done | bytes 1572880 | tf_op jit(solution)/shard_map/all_gather | solution.py:138
  982.2 2.8 copy.22
  985.0 2.6 gather_fusion.6
  987.6 2.6 multiply_convert_fusion.2
  990.3 2.3 convolution_multiply_fusion
  992.6 6.5 gather_fusion.3
  999.7 2.3 convolution_add_fusion.3
  1002.0 6.4 gather_fusion.7
  1008.4 6.4 broadcast_select_fusion
  1025.3 234.6 %all-reduce.13.cloned.1.call-done = (f32[128,6144]{1,0:T(8,128)}, f32[128,6144]{1,0:T(8,128)}) async-done(((f32[128,6144]{1,0:T(8,128)}, f32[128,6144]{1,0:T(8,128)}), (f32[128,6144]{1,0:T(8,128)}, f32[128,6144]{1,0:T(8,128)})) %all-reduce.13.cloned.1.call-update) | async-done | bytes 6291472
  1259.9 2.6 fusion.50
  (74 shorter events, 28.7 us)
Async XLA Ops:
  7.2 128.0 %copy-start = (bf16[1,6144,128]{2,1,0:T(8,128)(2,1)S(1)}, bf16[1,6144,128]{2,1,0:T(8,128)(2,1)}, u32[]{:S(2)}) copy-start(bf16[1,6144,128]{2,1,0:T(8,128)(2,1)} %param.16) | copy-start | bytes 4718596
  7.2 119.9 %all-gather.9.cloned.1.call-start = ((), (), s32[]{:S(2)}) async-start(), calls=%async_computation | async-start | bytes 3170304 | tf_op jit(solution)/shard_map/all_gather | solution.py:106
  8.7 369.8 %all-reduce.9.cloned.1.call-start = ((), (), s32[]{:S(2)}) async-start(), calls=%async_computation.4 | async-start | bytes 6291456
  132.5 2.6 copy-start.3
  149.8 0.7 copy-start.12
  149.8 1.5 copy-start.13
  149.8 228.8 %copy-start.11 = (bf16[1,1,6144]{2,1,0:T(2,128)(2,1)S(1)}, bf16[1,1,6144]{2,1,0:T(2,128)(2,1)}, u32[]{:S(2)}) copy-start(bf16[1,1,6144]{2,1,0:T(2,128)(2,1)} %param.13) | copy-start | bytes 36868
  149.8 345.5 %all-gather.13.cloned.1.call-start = ((), (), s32[]{:S(2)}) async-start(), calls=%async_computation.2 | async-start | bytes 3170304 | tf_op jit(solution)/shard_map/all_gather | solution.py:138
  151.2 461.2 %all-gather.11.cloned.1.call-start = ((), (), s32[]{:S(2)}) async-start(), calls=%async_computation.1 | async-start | bytes 3170304 | tf_op jit(solution)/shard_map/all_gather | solution.py:106
  380.1 6.1 collective-permute-start
  386.9 478.1 %all-reduce.11.cloned.1.call-start = ((), (), s32[]{:S(2)}) async-start(), calls=%async_computation.5 | async-start | bytes 6291456
  617.7 2.2 copy-start.1
  617.7 2.4 copy-start.6
  620.1 1.4 copy-start.4
  620.1 1.9 copy-start.8
  622.0 0.7 copy-start.14
  636.0 346.2 %all-gather.15.cloned.1.call-start = ((), (), s32[]{:S(2)}) async-start(), calls=%async_computation.3 | async-start | bytes 3170304 | tf_op jit(solution)/shard_map/all_gather | solution.py:138
  866.5 6.9 collective-permute-start.1
  874.0 385.9 %all-reduce.13.cloned.1.call-start = ((), (), s32[]{:S(2)}) async-start(), calls=%async_computation.6 | async-start | bytes 12582912
  987.6 2.7 copy-start.5
  992.6 6.5 copy-start.7
  1014.8 1.4 copy-start.2
  1016.8 1.4 copy-start.9
  1018.3 1.4 copy-start.10
Sparse Core Ops, SparseCore 0:
  12.2 114.7 all-gather.8
  149.9 228.6 all-reduce.8
  383.4 111.7 all-gather.12
  500.0 112.3 all-gather.10
  636.1 228.8 all-reduce.10
  874.2 108.0 all-gather.14
  1014.9 244.9 all-reduce.12
where the time goes:
time: 1270 us
  waiting for transfers between devices  1140 us (90%)
  local copies, waits for them, and re-layouts  54 us (4%)
  matrix products  28.6 us (2%)
  other arithmetic  26 us (2%)
  between operations  15.7 us (1%)
    unnamed x10, waiting for transfers between devices  690 us
    all_gather x2, waiting for transfers between devices, per_device(): gathered = lax.all_gather(current, 'et', axis=0, tiled=True)  225 us
    all_gather x2, waiting for transfers between devices, per_device(): grad_gathered = lax.all_gather(upstream, 'et', axis=0, tiled=True)  216 us
  transfers between devices with their start and end apart: 9, of which 9 were waited for; matrix products, arithmetic and copies ran while one was open for 2% of the time, Pallas kernels for 0%

commit v1 on v0

--- a/solution.py
+++ b/solution.py
@@ -103,7 +103,9 @@
         valid = (micro_raw >= 0) & (micro_raw < micro_count)
         micro_index = jnp.clip(micro_raw, 0, micro_count - 1)
         current = jnp.where(segment_index == 0, take_micro(inputs, micro_index), incoming)
-        gathered = lax.all_gather(current, "et", axis=0, tiled=True)
+        reply = jnp.stack([current for _ in range(lax.axis_size("et"))])
+        known = lax.all_to_all(reply, "et", 0, 0)
+        gathered = jnp.concatenate(known, axis=0)
         slot_rows, slot_scale, inverse = pick_route(
             route_rows, route_count, route_weight, micro_index
         )

time: 1270 us -> 1130 us (0.89)
  waiting for transfers between devices: 1140 us -> 919 us
  starting transfers between devices: 8.01 us -> 35.3 us
  local copies, waits for them, and re-layouts: 54 us -> 79.2 us
  other arithmetic: 26 us -> 44.1 us
    all_gather x2 -> x0, waiting for transfers between devices: 225 us -> none  [per_device(): gathered = lax.all_gather(current, 'et', axis=0, tiled=True)]
    all_to_all x0 -> x2, waiting for transfers between devices: none -> 37.9 us  [per_device(): known = lax.all_to_all(reply, 'et', 0, 0)]
    all_to_all x0 -> x2, starting transfers between devices: none -> 27.2 us  [per_device(): known = lax.all_to_all(reply, 'et', 0, 0)]
    all_gather x2, waiting for transfers between devices: 216 us -> 191 us  [per_device(): grad_gathered = lax.all_gather(upstream, 'et', axis=0, tiled=True)]
    another operation x0 -> x2, other arithmetic: none -> 22.5 us  [per_device(): reply = jnp.stack([current for _ in range(lax.axis_size('et'))])]
    unnamed x35 -> x43, local copies, waits for them, and re-layouts: 16.6 us -> 34.8 us
    unnamed x10 -> x8, waiting for transfers between devices: 690 us -> 685 us
  transfers between devices with their start and end apart: 9 -> 9, of which waited for: 9 -> 8; matrix products, arithmetic and copies ran while one was open for 2% -> 3% of each run, Pallas kernels for 0% -> 0%
where the time goes in v1:
time: 1130 us; the launch traced here: 1120 us
  waiting for transfers between devices  919 us (81%)
  local copies, waits for them, and re-layouts  79.2 us (7%)
  other arithmetic  44.1 us (4%)
  starting transfers between devices  35.3 us (3%)
  matrix products  28.6 us (3%)
  between operations  15.8 us (1%)
    unnamed x8, waiting for transfers between devices  685 us
    all_gather x2, waiting for transfers between devices, per_device(): grad_gathered = lax.all_gather(upstream, 'et', axis=0, tiled=True)  191 us
    all_to_all x2, waiting for transfers between devices, per_device(): known = lax.all_to_all(reply, 'et', 0, 0)  37.9 us
    unnamed x43, local copies, waits for them, and re-layouts  34.8 us
    all_to_all x2, starting transfers between devices, per_device(): known = lax.all_to_all(reply, 'et', 0, 0)  27.2 us
  transfers between devices with their start and end apart: 9, of which 8 were waited for; matrix products, arithmetic and copies ran while one was open for 3% of the time, Pallas kernels for 0%

profile of v1, /device:TPU:1, one launch (start us, length us, event | category | flops | bytes accessed | tf_op | source)
XLA Modules:
  0.0 1121.7 jit_solution(10390578793487919213)
XLA Ops:
  7.3 3.3 stack.7
  11.1 11.2 %reduce.4 = bf16[128,6144]{1,0:T(8,128)(2,1)S(1)} reduce(bf16[128,1,6144]{2,1,0:T(2,128)(2,1)} %stack.7, bf16[]{:T(256)} %broadcast.266), dimensions={1}, to_apply=%stack.7.reduce_sub_computation | reduce | bytes 3145730 | tf_op jit(solution)/shard_map/stack | solution.py:106
  24.4 16.7 %all-to-all-start = ((bf16[128,2,3072]{2,1,0:T(2,128)(2,1)}), bf16[128,2,3072]{2,1,0:T(2,128)(2,1)S(1)}, u32[]{:S(2)}, u32[]{:S(2)}) async-start(bf16[128,2,3072]{2,1,0:T(2,128)(2,1)} %reshape.326), calls=%async_computation | async-start | bytes 3145728 | tf_op jit(solution)/shard_map/all_to_all | solution.py:107
  43.5 37.9 %all-to-all-done = bf16[128,2,3072]{2,1,0:T(2,128)(2,1)S(1)} async-done(((bf16[128,2,3072]{2,1,0:T(2,128)(2,1)}), bf16[128,2,3072]{2,1,0:T(2,128)(2,1)S(1)}, u32[]{:S(2)}, u32[]{:S(2)}) %all-to-all-start) | async-done | bytes 1572896 | tf_op jit(solution)/shard_map/all_to_all | solution.py:107
  81.4 3.8 reshape.327
  85.2 2.8 copy.25
  88.0 2.6 gather_fusion
  93.2 4.2 convolution_multiply_fusion.1
  97.4 6.4 gather_fusion.1
  103.9 3.9 broadcast_select_fusion.3
  109.1 221.8 %all-reduce.9.cloned.1.call-done = f32[128,6144]{1,0:T(8,128)} async-done(((f32[128,6144]{1,0:T(8,128)}), f32[128,6144]{1,0:T(8,128)}) %all-reduce.9.cloned.1.call-update) | async-done | bytes 3145744
  334.9 3.7 collective-permute-done
  338.7 3.3 stack.8
  342.0 11.2 %reduce.5 = bf16[128,6144]{1,0:T(8,128)(2,1)S(1)} reduce(bf16[128,1,6144]{2,1,0:T(2,128)(2,1)} %stack.8, bf16[]{:T(256)} %broadcast.266), dimensions={1}, to_apply=%stack.8.reduce_sub_computation | reduce | bytes 3145730 | tf_op jit(solution)/shard_map/stack | solution.py:106
  355.3 10.5 all-to-all-start.1
  365.9 83.3 %all-gather.5.cloned.1.call-done = bf16[128,1,6144]{2,1,0:T(2,128)(2,1)} async-done(((bf16[1,1,6144]{2,1,0:T(2,128)(2,1)}), bf16[128,1,6144]{2,1,0:T(2,128)(2,1)}) %all-gather.5.cloned.1.call-update) | async-done | bytes 1572880 | tf_op jit(solution)/shard_map/all_gather | solution.py:140
  449.1 2.8 copy.23
  451.9 2.6 gather_fusion.4
  454.6 10.4 reshape.329
  464.9 2.8 copy.24
  478.1 6.5 gather_fusion.5
  484.5 4.0 broadcast_select_fusion.1
  488.6 228.8 %all-reduce.11.cloned.1.call-done = f32[128,6144]{1,0:T(8,128)} async-done(((f32[128,6144]{1,0:T(8,128)}), f32[128,6144]{1,0:T(8,128)}) %all-reduce.11.cloned.1.call-update) | async-done | bytes 3145744
  719.0 6.0 collective-permute-start.1
  726.8 107.9 %all-gather.7.cloned.1.call-done = bf16[128,1,6144]{2,1,0:T(2,128)(2,1)} async-done(((bf16[1,1,6144]{2,1,0:T(2,128)(2,1)}), bf16[128,1,6144]{2,1,0:T(2,128)(2,1)}) %all-gather.7.cloned.1.call-update) | async-done | bytes 1572880 | tf_op jit(solution)/shard_map/all_gather | solution.py:140
  834.8 2.8 copy.22
  840.2 2.6 multiply_convert_fusion.2
  845.1 6.5 gather_fusion.3
  854.5 6.4 gather_fusion.7
  860.9 6.4 broadcast_select_fusion
  877.8 234.3 %all-reduce.13.cloned.1.call-done = (f32[128,6144]{1,0:T(8,128)}, f32[128,6144]{1,0:T(8,128)}) async-done(((f32[128,6144]{1,0:T(8,128)}, f32[128,6144]{1,0:T(8,128)}), (f32[128,6144]{1,0:T(8,128)}, f32[128,6144]{1,0:T(8,128)})) %all-reduce.13.cloned.1.call-update) | async-done | bytes 6291472
  1112.1 2.6 fusion.50
  (85 shorter events, 45.8 us)
Async XLA Ops:
  7.2 86.1 %copy-start = (bf16[1,6144,128]{2,1,0:T(8,128)(2,1)S(1)}, bf16[1,6144,128]{2,1,0:T(8,128)(2,1)}, u32[]{:S(2)}) copy-start(bf16[1,6144,128]{2,1,0:T(8,128)(2,1)} %param.16) | copy-start | bytes 4718596
  24.4 18.0 %copy-start.14 = (s32[1,1,128]{2,1,0:T(1,128)S(1)}, s32[1,1,128]{2,1,0:T(1,128)}, u32[]{:S(2)}) copy-start(s32[1,1,128]{2,1,0:T(1,128)} %param.18) | copy-start | bytes 1540
  24.4 19.1 %copy-start.13 = (f32[1,1,128]{2,1,0:T(1,128)S(1)}, f32[1,1,128]{2,1,0:T(1,128)}, u32[]{:S(2)}) copy-start(f32[1,1,128]{2,1,0:T(1,128)} %param.20) | copy-start | bytes 1540
  24.4 57.1 %all-to-all-start = ((bf16[128,2,3072]{2,1,0:T(2,128)(2,1)}), bf16[128,2,3072]{2,1,0:T(2,128)(2,1)S(1)}, u32[]{:S(2)}, u32[]{:S(2)}) async-start(bf16[128,2,3072]{2,1,0:T(2,128)(2,1)} %reshape.326), calls=%async_computation | async-start | bytes 3145728 | tf_op jit(solution)/shard_map/all_to_all | solution.py:107
  41.0 289.8 %all-reduce.9.cloned.1.call-start = ((), (), s32[]{:S(2)}) async-start(), calls=%async_computation.4 | async-start | bytes 6291456
  90.6 2.6 copy-start.3
  107.8 0.7 copy-start.15
  107.8 223.1 %copy-start.11 = (bf16[1,1,6144]{2,1,0:T(2,128)(2,1)S(1)}, bf16[1,1,6144]{2,1,0:T(2,128)(2,1)}, u32[]{:S(2)}) copy-start(bf16[1,1,6144]{2,1,0:T(2,128)(2,1)} %param.13) | copy-start | bytes 36868
  107.8 226.4 %copy-start.12 = (bf16[1,1,6144]{2,1,0:T(2,128)(2,1)S(1)}, bf16[1,1,6144]{2,1,0:T(2,128)(2,1)}, u32[]{:S(2)}) copy-start(bf16[1,1,6144]{2,1,0:T(2,128)(2,1)} %param.14) | copy-start | bytes 36868
  107.8 341.3 %all-gather.5.cloned.1.call-start = ((), (), s32[]{:S(2)}) async-start(), calls=%async_computation.2 | async-start | bytes 3170304 | tf_op jit(solution)/shard_map/all_gather | solution.py:140
  332.5 6.1 collective-permute-start
  355.3 99.3 %all-to-all-start.1 = ((bf16[128,2,3072]{2,1,0:T(2,128)(2,1)}), bf16[128,2,3072]{2,1,0:T(2,128)(2,1)}, u32[]{:S(2)}, u32[]{:S(2)}) async-start(bf16[128,2,3072]{2,1,0:T(2,128)(2,1)} %reshape.328), calls=%async_computation.1 | async-start | bytes 3145728 | tf_op jit(solution)/shard_map/all_to_all | solution.py:107
  365.8 351.6 %all-reduce.11.cloned.1.call-start = ((), (), s32[]{:S(2)}) async-start(), calls=%async_computation.5 | async-start | bytes 6291456
  470.3 2.2 copy-start.1
  470.3 2.4 copy-start.6
  472.7 1.4 copy-start.4
  472.7 1.9 copy-start.8
  474.6 0.7 copy-start.16
  488.5 346.2 %all-gather.7.cloned.1.call-start = ((), (), s32[]{:S(2)}) async-start(), calls=%async_computation.3 | async-start | bytes 3170304 | tf_op jit(solution)/shard_map/all_gather | solution.py:140
  719.0 6.9 collective-permute-start.1
  726.6 385.6 %all-reduce.13.cloned.1.call-start = ((), (), s32[]{:S(2)}) async-start(), calls=%async_computation.6 | async-start | bytes 12582912
  840.2 2.7 copy-start.5
  845.1 6.5 copy-start.7
  867.3 1.4 copy-start.2
  869.4 1.4 copy-start.9
  870.8 1.4 copy-start.10
Sparse Core Ops, SparseCore 0:
  107.9 222.8 all-reduce.8
  335.7 113.3 all-gather.4
  488.7 228.7 all-reduce.10
  726.7 108.0 all-gather.6
  867.4 244.6 all-reduce.12
